TPU v7x, 32 devices: a whole 2x2x4 slice. The times are simulated.
32 devices in a mesh: rep: 16 (over z, x, core), shard: 2 (over y).
Axes of the slice: x: 2, y: 2, z: 4, core: 2. Of those that a mesh axis runs over, the one named last changes fastest.
Arguments:
- tokens: bfloat16 [32, 197, 512], P(('rep', 'shard')), may hold values from -6 to 6
- norm_one: bfloat16 [512], P('shard'), may hold values from 0.099609375 to 1.8984375
- w_qkv: bfloat16 [512, 1536], P('shard'), may hold values from -0.25 to 0.25
- w_attn: bfloat16 [512, 512], P('shard'), may hold values from -1 to 1
- norm_two: bfloat16 [512], P('shard'), may hold values from 0.099609375 to 1.8984375
- w_gate: bfloat16 [512, 4], P('shard'), may hold values from -0.1875 to 0.1875
- w_expin: bfloat16 [4, 512, 2048], P(None, 'shard'), may hold values from -0.25 to 0.25
- w_expout: bfloat16 [4, 2048, 512], P(None, 'shard'), may hold values from -0.125 to 0.125
- routes: int32 [32, 197, 2], P(('rep', 'shard')), may hold values from 0 to 3, all different within a row
- cotangent: bfloat16 [32, 197, 512], P(('rep', 'shard')), may hold values from -6 to 6
Outputs:
- output: bfloat16 [32, 197, 512], P(('rep', 'shard'))
- grad_tokens: bfloat16 [32, 197, 512], P(('rep', 'shard'))
- grad_norm_one: float32 [512], P('shard')
- grad_qkv: float32 [512, 1536], P('shard')
- grad_attn: float32 [512, 512], P('shard')
- grad_norm_two: float32 [512], P('shard')
- grad_gate: float32 [512, 4], P('shard')
- grad_expin: float32 [4, 512, 2048], P(None, 'shard')
- grad_expout: float32 [4, 2048, 512], P(None, 'shard')
Inputs may be any that keep to these rules, and one draw needn't show every extreme that they name: `routes`: each token names two different experts; every expert is named by some token.
All inputs are finite; a program needn't handle non-finite values.
Results may differ from a plain program's by a relative error of at most 0.024.
Values may be sent and summed in bfloat16 or wider, within the bound.
A program may use at most 192 MiB of HBM per device.

v0:
```python
from functools import partial

import jax
import jax.numpy as jnp
from jax import lax
from jax.sharding import PartitionSpec as P

HEADS = 8
HEAD_DIM = 64


norm_eps = 1e-06
highest = lax.Precision.HIGHEST
fdt = jnp.float32
bdt = jnp.bfloat16


def layer_norm(inputs, gain_vec):
    centre = inputs - jnp.mean(inputs, axis=-1, keepdims=True)
    variance = jnp.mean(centre * centre, axis=-1, keepdims=True)
    inv_root = lax.rsqrt(variance + norm_eps)
    normed = centre * inv_root
    return (normed * gain_vec, normed, inv_root)


def norm_back(grad_out, normed, inv_root, gain_vec):
    scaled = grad_out * gain_vec
    back = inv_root * (
        scaled
        - jnp.mean(scaled, axis=-1, keepdims=True)
        - normed * jnp.mean(scaled * normed, axis=-1, keepdims=True)
    )
    return (back, jnp.sum(grad_out * normed, axis=0))


def forward(weights, tokens, routes, kept_total):
    norm_one, w_qkv, w_attn, norm_two, w_gate, w_expin, w_expout = weights
    images, seq_len, model_width = tokens.shape
    tok_rows = images * seq_len
    resid = tokens.reshape(tok_rows, model_width).astype(fdt)
    hidden_one, normed_one, root_one = layer_norm(resid, norm_one.astype(fdt))
    hidden_one_low = hidden_one.astype(bdt)
    proj = jnp.dot(hidden_one_low, w_qkv, preferred_element_type=fdt).astype(bdt)
    proj = proj.reshape(images, seq_len, 3, HEADS, HEAD_DIM)
    queries = proj[:, :, 0]
    key_rows = proj[:, :, 1]
    val_rows = proj[:, :, 2]
    score_scale = HEAD_DIM ** (-0.5)
    scores = (
        jnp.einsum("ishd,ithd->ihst", queries, key_rows, preferred_element_type=fdt) * score_scale
    )
    if kept_total is None:
        log_total = jax.nn.logsumexp(scores, axis=-1, keepdims=True)
    else:
        log_total = kept_total
    soft_probs = jnp.exp(scores - log_total)
    probs_low = soft_probs.astype(bdt)
    attn_rows = jnp.einsum("ihst,ithd->ishd", probs_low, val_rows, preferred_element_type=fdt)
    attn_rows = attn_rows.reshape(tok_rows, model_width).astype(bdt)
    mixed = resid + jnp.dot(attn_rows, w_attn, preferred_element_type=fdt)
    gate_gain = norm_two.astype(fdt)
    hidden_two, normed_two, root_two = layer_norm(mixed, gate_gain)
    router = w_gate.astype(fdt)
    logits = jnp.dot(hidden_two, router, precision=highest)
    expert_count = router.shape[1]
    choose = (
        routes.reshape(tok_rows, 2)[:, :, None] == jnp.arange(expert_count)[None, None, :]
    ).astype(fdt)
    picked = jnp.sum(choose * logits[:, None, :], axis=-1)
    gates = jax.nn.softmax(picked, axis=-1)
    weight_map = jnp.sum(gates[:, :, None] * choose, axis=1)
    hidden_two_low = hidden_two.astype(bdt)
    expert_inner = jnp.einsum("td,edf->etf", hidden_two_low, w_expin, preferred_element_type=fdt)
    hidden_act = jax.nn.gelu(expert_inner, approximate=False).astype(bdt)
    outer = jnp.einsum("etf,efd->etd", hidden_act, w_expout, preferred_element_type=fdt)
    combined = mixed + jnp.sum(weight_map.T[:, :, None] * outer, axis=0)
    return {
        "combined": combined,
        "log_total": log_total,
        "resid": resid,
        "normed_one": normed_one,
        "root_one": root_one,
        "hidden_one_low": hidden_one_low,
        "queries": queries,
        "key_rows": key_rows,
        "val_rows": val_rows,
        "soft_probs": soft_probs,
        "probs_low": probs_low,
        "attn_rows": attn_rows,
        "normed_two": normed_two,
        "root_two": root_two,
        "hidden_two": hidden_two,
        "hidden_two_low": hidden_two_low,
        "choose": choose,
        "gates": gates,
        "weight_map": weight_map,
        "expert_inner": expert_inner,
        "hidden_act": hidden_act,
        "outer": outer,
    }


def on_device(
    tokens, norm_one, w_qkv, w_attn, norm_two, w_gate, w_expin, w_expout, routes, cotangent
):
    images, seq_len, model_width = tokens.shape
    tok_rows = images * seq_len
    whole = (
        lax.all_gather(norm_one, "shard", axis=0, tiled=True),
        lax.all_gather(w_qkv, "shard", axis=0, tiled=True),
        lax.all_gather(w_attn, "shard", axis=0, tiled=True),
        lax.all_gather(norm_two, "shard", axis=0, tiled=True),
        lax.all_gather(w_gate, "shard", axis=0, tiled=True),
        lax.all_gather(w_expin, "shard", axis=1, tiled=True),
        lax.all_gather(w_expout, "shard", axis=1, tiled=True),
    )
    first = forward(whole, tokens, routes, None)
    output = first["combined"].reshape(images, seq_len, model_width).astype(bdt)
    again = (
        lax.all_gather(norm_one, "shard", axis=0, tiled=True),
        lax.all_gather(w_qkv, "shard", axis=0, tiled=True),
        lax.all_gather(w_attn, "shard", axis=0, tiled=True),
        lax.all_gather(norm_two, "shard", axis=0, tiled=True),
        lax.all_gather(w_gate, "shard", axis=0, tiled=True),
        lax.all_gather(w_expin, "shard", axis=1, tiled=True),
        lax.all_gather(w_expout, "shard", axis=1, tiled=True),
    )
    parts = forward(again, tokens, routes, first["log_total"])
    g_one, m_qkv, m_attn, g_two, m_gate, m_expin, m_expout = again
    gain_one = g_one.astype(fdt)
    gain_two = g_two.astype(fdt)
    router = m_gate.astype(fdt)
    dout = cotangent.reshape(tok_rows, model_width).astype(fdt)
    dweight = jnp.sum(dout[None, :, :] * parts["outer"], axis=-1).T
    dout_exp = (parts["weight_map"].T[:, :, None] * dout[None, :, :]).astype(bdt)
    grad_expout = jnp.einsum(
        "etf,etd->efd", parts["hidden_act"], dout_exp, preferred_element_type=fdt
    )
    dhidden = jnp.einsum("etd,efd->etf", dout_exp, m_expout, preferred_element_type=fdt)
    gelu_exact = partial(jax.nn.gelu, approximate=False)
    _, gelu_pull = jax.vjp(gelu_exact, parts["expert_inner"])
    dinner = gelu_pull(dhidden)[0].astype(bdt)
    grad_expin = jnp.einsum(
        "td,etf->edf", parts["hidden_two_low"], dinner, preferred_element_type=fdt
    )
    dhidden_two = jnp.einsum("etf,edf->td", dinner, m_expin, preferred_element_type=fdt)
    choose = parts["choose"]
    gates = parts["gates"]
    dpicked = jnp.sum(choose * dweight[:, None, :], axis=-1)
    gate_dot = jnp.sum(gates * dpicked, axis=-1, keepdims=True)
    dpair = gates * (dpicked - gate_dot)
    dlogits = jnp.sum(dpair[:, :, None] * choose, axis=1)
    grad_gate = jnp.dot(parts["hidden_two"].T, dlogits, precision=highest)
    dhidden_two = dhidden_two + jnp.dot(dlogits, router.T, precision=highest)
    dmixed_norm, grad_norm_two = norm_back(
        dhidden_two, parts["normed_two"], parts["root_two"], gain_two
    )
    dmixed = dout + dmixed_norm
    dmixed_low = dmixed.astype(bdt)
    grad_attn = jnp.dot(parts["attn_rows"].T, dmixed_low, preferred_element_type=fdt)
    dattn = jnp.dot(dmixed_low, m_attn.T, preferred_element_type=fdt).astype(bdt)
    dattn = dattn.reshape(images, seq_len, HEADS, HEAD_DIM)
    dprobs = jnp.einsum("ishd,ithd->ihst", dattn, parts["val_rows"], preferred_element_type=fdt)
    dvalues = jnp.einsum("ihst,ishd->ithd", parts["probs_low"], dattn, preferred_element_type=fdt)
    soft_probs = parts["soft_probs"]
    row_delta = jnp.sum(dprobs * soft_probs, axis=-1, keepdims=True)
    dscores = (soft_probs * (dprobs - row_delta)).astype(bdt)
    score_scale = HEAD_DIM ** (-0.5)
    dqueries = (
        jnp.einsum("ihst,ithd->ishd", dscores, parts["key_rows"], preferred_element_type=fdt)
        * score_scale
    )
    dkeys = (
        jnp.einsum("ihst,ishd->ithd", dscores, parts["queries"], preferred_element_type=fdt)
        * score_scale
    )
    dproj = (
        jnp.stack([dqueries, dkeys, dvalues], axis=2).reshape(tok_rows, 3 * model_width).astype(bdt)
    )
    grad_qkv = jnp.dot(parts["hidden_one_low"].T, dproj, preferred_element_type=fdt)
    dhidden_one = jnp.dot(dproj, m_qkv.T, preferred_element_type=fdt)
    dresid_norm, grad_norm_one = norm_back(
        dhidden_one, parts["normed_one"], parts["root_one"], gain_one
    )
    grad_tokens = (dmixed + dresid_norm).reshape(images, seq_len, model_width).astype(bdt)
    owned = (
        lax.psum_scatter(
            grad_norm_one.astype(jnp.bfloat16), "shard", scatter_dimension=0, tiled=True
        ).astype(jnp.float32),
        lax.psum_scatter(
            grad_qkv.astype(jnp.bfloat16), "shard", scatter_dimension=0, tiled=True
        ).astype(jnp.float32),
        lax.psum_scatter(
            grad_attn.astype(jnp.bfloat16), "shard", scatter_dimension=0, tiled=True
        ).astype(jnp.float32),
        lax.psum_scatter(
            grad_norm_two.astype(jnp.bfloat16), "shard", scatter_dimension=0, tiled=True
        ).astype(jnp.float32),
        lax.psum_scatter(
            grad_gate.astype(jnp.bfloat16), "shard", scatter_dimension=0, tiled=True
        ).astype(jnp.float32),
        lax.psum_scatter(
            grad_expin.astype(jnp.bfloat16), "shard", scatter_dimension=1, tiled=True
        ).astype(jnp.float32),
        lax.psum_scatter(
            grad_expout.astype(jnp.bfloat16), "shard", scatter_dimension=1, tiled=True
        ).astype(jnp.float32),
    )
    summed = (
        lax.psum(owned[0].astype(jnp.bfloat16), "rep").astype(jnp.float32),
        lax.psum(owned[1].astype(jnp.bfloat16), "rep").astype(jnp.float32),
        lax.psum(owned[2].astype(jnp.bfloat16), "rep").astype(jnp.float32),
        lax.psum(owned[3].astype(jnp.bfloat16), "rep").astype(jnp.float32),
        lax.psum(owned[4].astype(jnp.bfloat16), "rep").astype(jnp.float32),
        lax.psum(owned[5].astype(jnp.bfloat16), "rep").astype(jnp.float32),
        lax.psum(owned[6].astype(jnp.bfloat16), "rep").astype(jnp.float32),
    )
    return (
        output,
        grad_tokens,
        summed[0],
        summed[1],
        summed[2],
        summed[3],
        summed[4],
        summed[5],
        summed[6],
    )


def solution(mesh):
    placed = (
        P(("rep", "shard"), None, None),
        P("shard"),
        P("shard", None),
        P("shard", None),
        P("shard"),
        P("shard", None),
        P(None, "shard", None),
        P(None, "shard", None),
        P(("rep", "shard"), None, None),
        P(("rep", "shard"), None, None),
    )
    return jax.shard_map(
        on_device,
        mesh=mesh,
        in_specs=placed,
        out_specs=(
            P(("rep", "shard"), None, None),
            P(("rep", "shard"), None, None),
            P("shard"),
            P("shard", None),
            P("shard", None),
            P("shard"),
            P("shard", None),
            P(None, "shard", None),
            P(None, "shard", None),
        ),
        check_vma=False,
    )
```

profile of v0, /device:TPU:0, one launch (start us, length us, event | category | flops | bytes accessed | tf_op | source)
XLA Modules:
  0.0 764.5 jit_solution(5038029769242780368)
XLA Ops:
  9.7 5.2 all-gather
  14.8 4.2 all-gather.1
  19.1 4.3 all_gather.32
  23.7 14.0 %all_gather.30 = bf16[512,512]{1,0:T(8,128)(2,1)} all-gather(bf16[256,512]{1,0:T(8,128)(2,1)S(1)} %copy-done.11), channel_id=1, replica_groups=mesh['rep'=16,'shard'=2] {'shard'}, dimensions={0}, use_global_device_ids=true | all-gather | bytes 786432 | tf_op jit(solution)/shard_map/all_gather | solution.py:111
  38.5 6.7 all-gather.6.cloned.1.call-done
  51.5 99.3 %all-gather.8.cloned.1.call-done = bf16[4,512,2048]{2,1,0:T(8,128)(2,1)} async-done(((bf16[4,256,2048]{2,1,0:T(8,128)(2,1)}), bf16[4,512,2048]{2,1,0:T(8,128)(2,1)}) %all-gather.8.cloned.1.call-update) | async-done | bytes 8388624 | tf_op jit(solution)/shard_map/all_gather | solution.py:114
  150.8 18.8 %fusion.2 = (bf16[4,197,2048]{2,1,0:T(8,128)(2,1)}, f32[4,197,2048]{2,1,0:T(8,128)}, f32[197,4,2048]{2,0,1:T(8,128)}) fusion(bf16[4,512,2048]{2,1,0:T(8,128)(2,1)} %all-gather.8.cloned.1.call-done, f32[512]{0:T(512)S(1)} %bitcast.219, f32[197]{0:T(256)S(1)} %add_rsqrt_fusion, f32[197,512]{1,0:T(8,128)S(1)} %get-tuple-element.69, ...), kind=kOutput, calls=%fused_computation.10 | convolution fusion | flops 1757857792 | bytes 24933928 | tf_op jit(solution)/shard_map/td,edf->etf/dot_general | solution.py:73
  169.6 86.8 %all-gather.10.cloned.1.call-done = bf16[4,2048,512]{2,1,0:T(8,128)(2,1)} async-done(((bf16[4,1024,512]{2,1,0:T(8,128)(2,1)}), bf16[4,2048,512]{2,1,0:T(8,128)(2,1)}) %all-gather.10.cloned.1.call-update) | async-done | bytes 8388624 | tf_op jit(solution)/shard_map/all_gather | solution.py:115
  256.4 6.5 multiply_reduce_fusion.1
  263.0 11.2 %fusion.8 = bf16[4,197,2048]{2,1,0:T(8,128)(2,1)S(1)} fusion(f32[4,197,2048]{2,1,0:T(8,128)} %get-tuple-element.63, f32[197,4,2048]{2,0,1:T(8,128)} %get-tuple-element.70, bf16[4,2048,512]{2,1,0:T(8,128)(2,1)} %all-gather.10.cloned.1.call-done, f32[197,512]{1,0:T(8,128)S(1)} %copy-done.6, f32[4,197]{1,0:T(4,128)S(1)} %bitcast.233), kind=kOutput, calls=%fused_computation.16 | convolution fusion | flops 1675956224 | bytes 24933456 | tf_op jit(solution)/shard_map/etd,efd->etf/dot_general | solution.py:139
  274.3 7.4 convolution_bitcast_fusion.1
  287.0 2.6 multiply_reduce_fusion
  295.0 8.1 %convert_bitcast_fusion = bf16[4,512,2048]{1,2,0:T(8,128)(2,1)} fusion(bf16[4,197,2048]{2,1,0:T(8,128)(2,1)} %copy-done.1, f32[512]{0:T(512)S(1)} %bitcast.222, f32[197,512]{1,0:T(8,128)S(1)} %get-tuple-element.69, f32[197]{0:T(256)S(1)} %add_rsqrt_fusion, f32[197]{0:T(256)S(1)} %broadcast_multiply_fusion.4), kind=kOutput, calls=%fused_computation.1 | convolution fusion | flops 1657153536 | bytes 12023336 | tf_op jit(solution)/shard_map/td,etf->edf/dot_general | solution.py:143
  304.1 7.9 %convolution_convert_fusion = bf16[4,2048,512]{2,1,0:T(8,128)(2,1)} fusion(bf16[4,197,2048]{2,1,0:T(8,128)(2,1)} %get-tuple-element.62, f32[197,512]{1,0:T(8,128)S(1)} %copy-done.7, f32[4,197]{1,0:T(4,128)S(1)} %bitcast.234), kind=kOutput, calls=%fused_computation.30 | convolution fusion | flops 1657556992 | bytes 12022864 | tf_op jit(solution)/shard_map/etf,etd->efd/dot_general | solution.py:136
  313.4 19.7 %reduce-scatter.8.cloned.1.call-done = bf16[256,1536]{1,0:T(8,128)(2,1)} async-done(((bf16[512,1536]{1,0:T(8,128)(2,1)}), bf16[256,1536]{1,0:T(8,128)(2,1)}) %reduce-scatter.8.cloned.1.call-update) | async-done | bytes 786448 | tf_op jit(solution)/shard_map/reduce_scatter | solution.py:190
  333.2 102.0 %reduce-scatter.12.cloned.1.call-done = bf16[4,256,2048]{1,2,0:T(8,128)(2,1)} async-done(((bf16[4,512,2048]{1,2,0:T(8,128)(2,1)}), bf16[4,256,2048]{1,2,0:T(8,128)(2,1)}) %reduce-scatter.12.cloned.1.call-update) | async-done | bytes 4194320 | tf_op jit(solution)/shard_map/reduce_scatter | solution.py:202
  435.2 102.2 %reduce-scatter.14.cloned.1.call-done = bf16[4,1024,512]{2,1,0:T(8,128)(2,1)} async-done(((bf16[4,2048,512]{2,1,0:T(8,128)(2,1)}), bf16[4,1024,512]{2,1,0:T(8,128)(2,1)}) %reduce-scatter.14.cloned.1.call-update) | async-done | bytes 4194320 | tf_op jit(solution)/shard_map/reduce_scatter | solution.py:205
  539.5 4.9 all-reduce.4
  545.5 4.4 reduce-scatter.16.cloned.1.call-done
  550.9 34.5 %all-reduce.2 = (bf16[256]{0:T(256)(128)(2,1)S(1)}, bf16[256]{0:T(256)(128)(2,1)S(1)}, bf16[256,4]{0,1:T(4,128)(2,1)S(1)}) all-reduce(bf16[256]{0:T(256)(128)(2,1)S(1)} %dynamic-slice.1, bf16[256]{0:T(256)(128)(2,1)S(1)} %dynamic-slice.3, bf16[256,4]{0,1:T(4,128)(2,1)S(1)} %copy.62), channel_id=1, replica_groups=mesh['rep'=16,'shard'=2] {'rep'}, use_global_device_ids=true, to_apply=%region_22.0 | all-reduce | flops 1536 | bytes 6144 | tf_op jit(solution)/shard_map/psum | solution.py:210
  587.1 153.0 %all-reduce.7.cloned.1.call-done = (bf16[4,256,2048]{1,2,0:T(8,128)(2,1)}, bf16[256,1536]{1,0:T(8,128)(2,1)}, bf16[256,512]{1,0:T(8,128)(2,1)}, bf16[4,1024,512]{2,1,0:T(8,128)(2,1)}) async-done(((bf16[4,256,2048]{1,2,0:T(8,128)(2,1)}, bf16[256,1536]{1,0:T(8,128)(2,1)}, bf16[256,512]{1,0:T(8,128)(2,1)}, bf16[4,1024,512]{2,1,0:T(8,128)(2,1)}), (bf16[4,256,2048]{1,2,0:T(8,128)(2,1)}, ...) | async-done | bytes 9437200 | tf_op jit(solution)/shard_map/psum | solution.py:215
  740.0 2.5 convert_element_type.206
  744.3 6.9 copy.56
  751.2 6.8 convert_element_type.217
  (109 shorter events, 29.7 us)
Async XLA Ops:
  7.2 2.3 copy-start
  7.2 2.4 copy-start.14
  7.2 7.6 copy-start.15
  7.2 11.9 %copy-start.13 = (bf16[256,4]{0,1:T(4,128)(2,1)S(1)}, bf16[256,4]{0,1:T(4,128)(2,1)}, u32[]{:S(2)}) copy-start(bf16[256,4]{0,1:T(4,128)(2,1)} %param.15) | copy-start | bytes 6148
  7.2 16.4 %copy-start.11 = (bf16[256,512]{1,0:T(8,128)(2,1)S(1)}, bf16[256,512]{1,0:T(8,128)(2,1)}, u32[]{:S(2)}) copy-start(bf16[256,512]{1,0:T(8,128)(2,1)} %param.13) | copy-start | bytes 786436
  7.2 30.5 %copy-start.9 = (bf16[1,197,512]{2,1,0:T(8,128)(2,1)S(1)}, bf16[1,197,512]{2,1,0:T(8,128)(2,1)}, u32[]{:S(2)}) copy-start(bf16[1,197,512]{2,1,0:T(8,128)(2,1)} %param.19) | copy-start | bytes 605188
  7.2 38.0 %all-gather.6.cloned.1.call-start = ((), (), s32[]{:S(2)}) async-start(), calls=%async_computation.5 | async-start | bytes 2359296 | tf_op jit(solution)/shard_map/all_gather | solution.py:110
  8.0 142.8 %all-gather.8.cloned.1.call-start = ((), (), s32[]{:S(2)}) async-start(), calls=%async_computation.6 | async-start | bytes 12582912 | tf_op jit(solution)/shard_map/all_gather | solution.py:114
  8.7 247.7 %all-gather.10.cloned.1.call-start = ((), (), s32[]{:S(2)}) async-start(), calls=%async_computation.7 | async-start | bytes 12582912 | tf_op jit(solution)/shard_map/all_gather | solution.py:115
  9.5 304.0 %reduce-scatter.10.cloned.1.call-start = ((), (), s32[]{:S(2)}) async-start(), calls=%async_computation.9 | async-start | bytes 786432 | tf_op jit(solution)/shard_map/reduce_scatter | solution.py:193
  23.7 27.7 %copy-start.12 = (s32[1,197,2]{1,2,0:T(2,128)S(1)}, s32[1,197,2]{1,2,0:T(2,128)}, u32[]{:S(2)}) copy-start(s32[1,197,2]{1,2,0:T(2,128)} %param.18) | copy-start | bytes 4732
  51.5 204.9 %copy-start.6 = (f32[197,512]{1,0:T(8,128)S(1)}, f32[197,512]{1,0:T(8,128)}, u32[]{:S(2)}) copy-start(f32[197,512]{1,0:T(8,128)} %bitcast_convert_fusion) | copy-start | bytes 1210372
  274.2 7.5 copy-start.1
  274.2 8.1 %copy-start.10 = (bf16[1,197,512]{2,1,0:T(8,128)(2,1)S(1)}, bf16[1,197,512]{2,1,0:T(8,128)(2,1)}, u32[]{:S(2)}) copy-start(bf16[1,197,512]{2,1,0:T(8,128)(2,1)} %param.19) | copy-start | bytes 605188
  274.2 8.9 %copy-start.2 = (bf16[512,512]{1,0:T(8,128)(2,1)S(1)}, bf16[512,512]{1,0:T(8,128)(2,1)}, u32[]{:S(2)}) copy-start(bf16[512,512]{1,0:T(8,128)(2,1)} %all_gather.30) | copy-start | bytes 1572868
  274.2 9.9 %copy-start.4 = (bf16[8,64,197]{2,1,0:T(8,128)(2,1)S(1)}, bf16[8,64,197]{2,1,0:T(8,128)(2,1)}, u32[]{:S(2)}) copy-start(bf16[8,64,197]{2,1,0:T(8,128)(2,1)} %copy-done.3) | copy-start | bytes 605188
  289.6 43.6 %reduce-scatter.8.cloned.1.call-start = ((), (), s32[]{:S(2)}) async-start(), calls=%async_computation.8 | async-start | bytes 2359296 | tf_op jit(solution)/shard_map/reduce_scatter | solution.py:190
  289.8 2.6 copy-start.5
  294.9 140.2 %reduce-scatter.12.cloned.1.call-start = ((), (), s32[]{:S(2)}) async-start(), calls=%async_computation.10 | async-start | bytes 12582912 | tf_op jit(solution)/shard_map/reduce_scatter | solution.py:202
  303.1 234.3 %reduce-scatter.14.cloned.1.call-start = ((), (), s32[]{:S(2)}) async-start(), calls=%async_computation.11 | async-start | bytes 12582912 | tf_op jit(solution)/shard_map/reduce_scatter | solution.py:205
  312.0 225.4 %copy-start.16 = (u32[32]{0:T(128)S(1)}, u32[32]{0:T(128)}, u32[]{:S(2)}) copy-start(u32[32]{0:T(128)} %constant.92) | copy-start | bytes 388
  312.0 226.7 %copy-start.8 = (bf16[512,1536]{1,0:T(8,128)(2,1)S(1)}, bf16[512,1536]{1,0:T(8,128)(2,1)}, u32[]{:S(2)}) copy-start(bf16[512,1536]{1,0:T(8,128)(2,1)} %all-gather.6.cloned.1.call-done) | copy-start | bytes 4718596
  312.0 237.9 %reduce-scatter.16.cloned.1.call-start = ((), (), s32[]{:S(2)}) async-start(), calls=%async_computation.12 | async-start | bytes 196608
  313.3 426.7 %all-reduce.7.cloned.1.call-start = ((), (), s32[]{:S(2)}) async-start(), calls=%async_computation.13 | async-start | bytes 18874368 | tf_op jit(solution)/shard_map/psum | solution.py:215
  (2 other events, 1.7 us)
Sparse Core Ops, SparseCore 0:
  9.6 35.5 all-gather.5
  46.7 103.9 all-gather.7
  152.3 103.9 all-gather.9
  289.7 14.5 reduce-scatter.9
  307.0 26.0 reduce-scatter.7
  335.9 99.2 reduce-scatter.11
  438.1 99.2 reduce-scatter.13
  539.6 10.2 reduce-scatter.15
  553.9 186.0 all-reduce.6
where the time goes:
time: 765 us; the launch traced here: 764 us
  waiting for transfers between devices  576 us (75%)
  matrix products  74.1 us (10%)
  blocking collectives  67.2 us (9%)
  other arithmetic  18.4 us (2%)
  between operations  14.8 us (2%)
  local copies, waits for them, and re-layouts  13.1 us (2%)
    psum x1, waiting for transfers between devices, on_device(): lax.psum(owned[5].astype(jnp.bfloat16), 'rep').astype(jnp.float32)  153 us
    reduce_scatter x1, waiting for transfers between devices, on_device(): lax.psum_scatter(grad_expout.astype(jnp.bfloat16), 'shard', scatter_dimen...  102 us
    reduce_scatter x1, waiting for transfers between devices, on_device(): lax.psum_scatter(grad_expin.astype(jnp.bfloat16), 'shard', scatter_dimens...  102 us
    all_gather x1, waiting for transfers between devices, on_device(): lax.all_gather(w_expin, 'shard', axis=1, tiled=True)  99.3 us
    all_gather x1, waiting for transfers between devices, on_device(): lax.all_gather(w_expout, 'shard', axis=1, tiled=True)  86.8 us
    psum x1, blocking collectives, on_device(): lax.psum(owned[0].astype(jnp.bfloat16), 'rep').astype(jnp.float32)  34.5 us
    reduce_scatter x1, waiting for transfers between devices, on_device(): lax.psum_scatter(grad_qkv.astype(jnp.bfloat16), 'shard', scatter_dimensio...  19.7 us
    dot_general x1, matrix products, forward(): jnp.einsum('td,edf->etf', hidden_two_low, w_expin, preferred_element_type...  18.8 us
  transfers between devices with their start and end apart: 9, of which 8 were waited for; matrix products, arithmetic and copies ran while one was open for 7% of the time, Pallas kernels for 0%

commit v1 on v0

v1 whole, which is shorter than its diff:
```python
from functools import partial
from types import SimpleNamespace

import jax
import jax.numpy as jnp
from jax import lax
from jax.experimental import pallas as pl
from jax.experimental.pallas import tpu as pltpu
from jax.sharding import PartitionSpec as P

HEADS = 8
HEAD_DIM = 64
GROUP = 8
NORM_EPS = 1e-06
MESH = pl.DeviceIdType.MESH
f32 = jnp.float32
bf16 = jnp.bfloat16
VMEM_BYTES = 60 << 20


def nn(a, b):
    return lax.dot_general(a, b, (((1,), (0,)), ((), ())), preferred_element_type=f32)


def nt(a, b):
    return lax.dot_general(a, b, (((1,), (1,)), ((), ())), preferred_element_type=f32)


def tn(a, b):
    return lax.dot_general(a, b, (((0,), (0,)), ((), ())), preferred_element_type=f32)


def split3(v):
    a = v.astype(bf16)
    r = v - a.astype(f32)
    b = r.astype(bf16)
    c = (r - b.astype(f32)).astype(bf16)
    return a, b, c


def geometry(mesh, tokens_shape, ff):
    g = SimpleNamespace()
    g.R, g.S = mesh.shape["rep"], mesh.shape["shard"]
    g.T = GROUP // g.S
    g.L = g.R // g.T
    g.C = min(g.T, 2)
    g.X = g.T // g.C
    g.seq = tokens_shape[1]
    g.TP = -(-g.seq // 16) * 16
    g.TK = -(-g.seq // 128) * 128
    g.ff = ff
    g.U = ff // GROUP
    g.CR = min(128, g.U, 512 // g.S)
    return g


class Where:
    def __init__(self, g):
        self.g = g
        self.rep = lax.axis_index("rep")
        self.s = lax.axis_index("shard")
        self.t = lax.rem(self.rep, g.T)
        self.red = self.rep // g.T
        self.x = self.t // g.C
        self.c = lax.rem(self.t, g.C)
        self.tp = self.s * g.T + self.t

    def sj(self, j):
        return lax.rem(self.s + j, self.g.S)

    def xj(self, j):
        return lax.rem(self.x + j, self.g.X)

    def cj(self, j):
        return lax.rem(self.c + j, self.g.C)

    def block(self, js, jx, jc):
        return self.sj(js) * self.g.T + self.xj(jx) * self.g.C + self.cj(jc)

    def dev(self, js=0, jx=0, jc=0):
        return (self.red * self.g.T + self.xj(jx) * self.g.C + self.cj(jc), self.sj(js))


def greet(w, chain):
    g = w.g
    bar = pltpu.get_barrier_semaphore()
    n = 0
    for js in range(g.S):
        for jx in range(g.X):
            for jc in range(g.C):
                if js or jx or jc:
                    pl.semaphore_signal(bar, inc=1, device_id=w.dev(js, jx, jc), device_id_type=MESH)
                    n += 1
    if chain and g.L > 1:
        @pl.when(w.red > 0)
        def _():
            pl.semaphore_signal(bar, inc=1, device_id=(w.rep - g.T, w.s), device_id_type=MESH)

        @pl.when(w.red < g.L - 1)
        def _():
            pl.semaphore_signal(bar, inc=1, device_id=(w.rep + g.T, w.s), device_id_type=MESH)

        n = n + (w.red > 0).astype(jnp.int32) + (w.red < g.L - 1).astype(jnp.int32)
    pl.semaphore_wait(bar, n)


class Sends:
    def __init__(self, sem):
        self.sem, self.n, self.open = sem, 0, []

    def go(self, src, dst, recv, dev):
        cp = pltpu.make_async_remote_copy(
            src_ref=src, dst_ref=dst, send_sem=self.sem.at[self.n], recv_sem=recv,
            device_id=dev, device_id_type=MESH,
        )
        self.n += 1
        cp.start()
        self.open.append(cp)
        return cp

    def finish(self):
        for cp in self.open:
            cp.wait_send()
        self.open = []


def arrived(ref, sem):
    pltpu.make_async_copy(ref, ref, sem).wait()


def gather_group(w, sends, at, sem, halves):
    g = w.g
    first, second = halves
    own = w.block(0, 0, 0)

    def send(js, jx, half, to):
        b = w.block(js, jx, 0)
        sends.go(at(b, half), at(b, half), sem.at[b, half], w.dev(*to))

    def core(js, jx, half):
        for j in range(1, g.C):
            send(js, jx, half, (0, 0, j))

    def wait(js, jx, jc, half):
        b = w.block(js, jx, jc)
        arrived(at(b, half), sem.at[b, half])

    for j in range(1, g.X):
        send(0, 0, first, (0, j))
    for j in range(1, g.S):
        send(0, 0, second, (j,))
    for j in range(1, g.S):
        send(0, 0, first, (j,))
    for j in range(1, g.X):
        send(0, 0, second, (0, j))
    core(0, 0, first)
    core(0, 0, second)
    for i in range(1, g.X):
        wait(0, i, 0, first)
        for j in range(1, g.S):
            send(0, i, first, (j,))
        core(0, i, first)
    for i in range(1, g.S):
        wait(i, 0, 0, second)
        for j in range(1, g.X):
            send(i, 0, second, (0, j))
        core(i, 0, second)
    for js in range(1, g.S):
        for jx in range(g.X):
            wait(js, jx, 0, first)
            core(js, jx, first)
    for jx in range(1, g.X):
        for js in range(g.S):
            wait(js, jx, 0, second)
            core(js, jx, second)
    for jc in range(1, g.C):
        for js in range(g.S):
            for jx in range(g.X):
                wait(js, jx, jc, first)
                wait(js, jx, jc, second)


def layer_norm(v, gain):
    c = v - jnp.mean(v, axis=-1, keepdims=True)
    r = lax.rsqrt(jnp.mean(c * c, axis=-1, keepdims=True) + NORM_EPS)
    xhat = c * r
    return xhat * gain, xhat, r


def norm_back(dh, xhat, r, gain):
    d = dh * gain
    return r * (
        d - jnp.mean(d, axis=-1, keepdims=True) - xhat * jnp.mean(d * xhat, axis=-1, keepdims=True)
    )


def padded(ref, rows):
    v = ref[0].astype(f32)
    return jnp.concatenate([v, jnp.zeros((rows - v.shape[0], v.shape[1]), f32)], axis=0)


def rows_of_small(small):
    pick = (
        lax.broadcasted_iota(jnp.int32, (8, 128), 0) == lax.broadcasted_iota(jnp.int32, (8, 128), 1)
    ).astype(f32).astype(bf16)
    return nt(pick, small)


def turned(v):
    r, c = v.shape
    pr, pc = -(-r // 128) * 128 - r, -(-c // 128) * 128 - c
    if pc:
        v = jnp.concatenate([v, jnp.zeros((r, pc), f32)], axis=1)
    if pr:
        v = jnp.concatenate([v, jnp.zeros((pr, v.shape[1]), f32)], axis=0)
    return v.T


def gates_of(h2, small_rows, routes_t):
    wt = small_rows.astype(bf16)
    a, b, c = split3(h2)
    logits = nt(wt, a) + nt(wt, b) + nt(wt, c)
    row = lax.broadcasted_iota(jnp.int32, logits.shape, 0).astype(f32)
    pick0 = (row == routes_t[0:1]).astype(f32)
    pick1 = (row == routes_t[1:2]).astype(f32)
    p0 = jnp.sum(pick0 * logits, axis=0, keepdims=True)
    p1 = jnp.sum(pick1 * logits, axis=0, keepdims=True)
    m = jnp.maximum(p0, p1)
    e0 = jnp.exp(p0 - m)
    e1 = jnp.exp(p1 - m)
    tot = e0 + e1
    return pick0 * (e0 / tot) + pick1 * (e1 / tot)


def attention(proj, attn, probs, g):
    D = attn.shape[1]
    low = lax.broadcasted_iota(jnp.int32, (1, 128), 1) < HEAD_DIM
    keep = lax.broadcasted_iota(jnp.int32, (1, g.TK), 1) < g.seq
    zero = jnp.zeros((), bf16)
    for p in range(D // 128):
        q2 = proj[0 : g.TP, p * 128 : (p + 1) * 128] * jnp.asarray(HEAD_DIM**-0.5, bf16)
        k2 = proj[:, D + p * 128 : D + (p + 1) * 128]
        v2 = proj[:, 2 * D + p * 128 : 2 * D + (p + 1) * 128]
        out = None
        for i in range(2):
            mine = low if i == 0 else jnp.logical_not(low)
            s = nt(jnp.where(mine, q2, zero), k2)
            s = jnp.where(keep, s, -jnp.inf)
            e = jnp.exp(s - jnp.max(s, axis=-1, keepdims=True))
            pr = e * (1.0 / jnp.sum(e, axis=-1, keepdims=True))
            probs[2 * p + i] = pr
            o = nn(pr.astype(bf16), jnp.where(mine, v2, zero))
            out = o if out is None else out + o
        attn[:, p * 128 : (p + 1) * 128] = out.astype(bf16)


def front(g, experts, ins, outs, scr):
    w = Where(g)
    tok, cot, routes, small, wqkv_h, wattn_h, wexpin_h = ins
    H, DO, WM, win, wqkv, wattn, smallf, proj, attn, probs, mixed = outs
    ssem, rsem, hsem, dsem, msem, lsem = scr
    D = tok.shape[2]
    Ds = D // g.S
    greet(w, False)
    sends = Sends(ssem)

    part = Ds // g.C
    local = []

    def rows(ref, s, lo, n):
        return ref.at[pl.ds(pl.multiple_of(s * Ds + lo, 16), n)]

    mine = pl.multiple_of(w.c * part, 16)

    def weight_out(i, src, dst):
        for j in range(1, g.S):
            d = dst.at[pl.ds(pl.multiple_of(w.s * Ds + mine, 16), part)]
            sends.go(src.at[pl.ds(mine, part)], d, rsem.at[i, w.s, w.c], w.dev(js=j))

    def weight_in(i, dst):
        for j in range(1, g.S):
            o = w.sj(j)
            d = dst.at[pl.ds(pl.multiple_of(o * Ds + mine, 16), part)]
            arrived(d, rsem.at[i, o, w.c])
            for k in range(1, g.C):
                sends.go(d, d, rsem.at[i, o, w.c], w.dev(jc=k))

    def weight_core(i, dst):
        for j in range(1, g.S):
            for k in range(1, g.C):
                o = w.sj(j)
                m = pl.multiple_of(o * Ds + w.cj(k) * part, 16)
                arrived(dst.at[pl.ds(m, part)], rsem.at[i, o, w.cj(k)])

    for i, (src, dst) in enumerate(((small, smallf), (wqkv_h, wqkv), (wattn_h, wattn))):
        weight_out(i, src, dst)
        cp = pltpu.make_async_copy(src, dst.at[pl.ds(pl.multiple_of(w.s * Ds, 16), Ds)], lsem.at[i])
        cp.start()
        local.append(cp)

    def expin_cp(src, owner, e, target):
        return (
            wexpin_h.at[e, :, pl.ds(pl.multiple_of(target * g.U, 128), g.U)],
            win.at[pl.ds(pl.multiple_of(owner * Ds, 16), Ds), e * g.U : (e + 1) * g.U],
        )

    for e in range(experts):
        src, dst = expin_cp(wexpin_h, w.s, e, w.tp)
        cp = pltpu.make_async_copy(src, dst, lsem.at[3 + e])
        cp.start()
        local.append(cp)

    def at(buf, n):
        def view(b, half):
            lo, size = ((0, n), (n, g.TP - n))[half]
            return buf.at[pl.ds(pl.multiple_of(b * g.TP + lo, 16), size)]
        return view

    own = pl.ds(pl.multiple_of(w.tp * g.TP, 16), g.TP)
    DO[own] = padded(cot, g.TP).astype(bf16)

    rt = routes[0].astype(f32)
    rt = jnp.concatenate([rt, jnp.full((g.TP - g.seq, 2), -1.0, f32)], axis=0)
    routes_t = turned(rt)[0:8, 0 : g.TP]
    resid = padded(tok, g.TP)
    c = resid - jnp.mean(resid, axis=-1, keepdims=True)
    xhat = c * lax.rsqrt(jnp.mean(c * c, axis=-1, keepdims=True) + NORM_EPS)

    for i, dst in enumerate((smallf, wqkv, wattn)):
        weight_in(i, dst)
    for cp in local[:2]:
        cp.wait()
    for i, dst in enumerate((smallf, wqkv, wattn)):
        weight_core(i, dst)
    for j in range(1, g.S):
        for e in range(experts):
            target = w.sj(j) * g.T + w.t
            src, dst = expin_cp(wexpin_h, w.s, e, target)
            sends.go(src, dst, lsem.at[8 + w.s * experts + e], w.dev(js=j))
    half0 = g.TP // 32 * 16
    small_rows = rows_of_small(smallf[...])
    gain_one = small_rows[experts : experts + 1]
    h1 = (xhat * gain_one).astype(bf16)
    for k in range(3):
        proj[0 : g.TP, k * D : (k + 1) * D] = nn(h1, wqkv[:, k * D : (k + 1) * D]).astype(bf16)
    if g.TK > g.TP:
        proj[g.TP : g.TK] = jnp.zeros((g.TK - g.TP, 3 * D), bf16)
    attention(proj, attn, probs, g)
    gather_group(w, sends, at(DO, half0), dsem, (0, 1))
    local[2].wait()
    mx = resid + nn(attn[...], wattn[...])
    mixed[...] = mx
    h2, _, _ = layer_norm(mx, small_rows[experts + 1 : experts + 2])
    H[own] = h2.astype(bf16)
    WM[w.tp] = jnp.zeros((8, g.TK), f32)
    WM[w.tp, :, 0 : g.TP] = gates_of(h2, small_rows, routes_t)
    gather_group(w, sends, at(H, half0), hsem, (0, 1))

    for js in range(g.S):
        for jx in range(g.X):
            for jc in range(g.C):
                if js or jx or jc:
                    sends.go(WM.at[w.tp], WM.at[w.tp], msem.at[w.tp], w.dev(js, jx, jc))
    for js in range(g.S):
        for jx in range(g.X):
            for jc in range(g.C):
                if js or jx or jc:
                    b = w.block(js, jx, jc)
                    arrived(WM.at[b], msem.at[b])
    for cp in local[3:]:
        cp.wait()
    for j in range(1, g.S):
        for e in range(experts):
            o = w.sj(j)
            _, dst = expin_cp(wexpin_h, o, e, w.tp)
            arrived(dst, lsem.at[8 + o * experts + e])
    sends.finish()


def erf_parts(v):
    av = jnp.abs(v)
    t = 1.0 / (1.0 + av * (0.3275911 * 0.7071067811865476))
    e = jnp.exp(v * v * -0.5)
    poly = t * (0.5 * 0.254829592 + t * (0.5 * -0.284496736 + t * (0.5 * 1.421413741 + t * (0.5 * -1.453152027 + t * (0.5 * 1.061405429)))))
    q = poly * e
    return jnp.where(v > 0, 1.0 - q, q), e * 0.3989422804014327


def middle(g, experts, ins, outs, scr):
    H, DO, WM, win, wout_h = ins
    PO, PH, DW, GO, GI = outs
    wout, INN, ACT, DG, DIN, COL, sem = scr
    w = Where(g)
    n = g.TP
    U, D = g.U, H.shape[1]
    RT = 16
    cps = []
    for e in range(experts):
        cp = pltpu.make_async_copy(
            wout_h.at[e, pl.ds(pl.multiple_of(w.t * U, 16), U)], wout.at[pl.ds(e * U, U)], sem.at[e]
        )
        cp.start()
        cps.append(cp)

    def rows(b):
        return pl.ds(pl.multiple_of(b * n, 16), n)

    @pl.loop(0, GROUP)
    def _(b):
        INN[...] = nn(H[rows(b)], win[...])
        COL[...] = turned(WM[b])

        @pl.loop(0, n // RT)
        def _(i):
            r = pl.ds(pl.multiple_of(i * RT, RT), RT)
            o = pl.ds(pl.multiple_of(b * n + i * RT, RT), RT)
            for e in range(experts):
                v = INN[r, e * U : (e + 1) * U]
                cdf, pdf = erf_parts(v)
                gate = COL[r, e : e + 1]
                ACT[o, e * U : (e + 1) * U] = (v * cdf * gate).astype(bf16)
                DG[o, e * U : (e + 1) * U] = (cdf + v * pdf) * gate

    for cp in cps:
        cp.wait()
    for e in range(experts):
        v = tn(ACT[:, e * U : (e + 1) * U], DO[...])
        k = 0
        for u in range(U // g.CR):
            for c in range(D // 256):
                GO[e * (U // g.CR) * (D // 256) + k] = v[u * g.CR : (u + 1) * g.CR, c * 256 : (c + 1) * 256]
                k += 1

    @pl.loop(0, GROUP)
    def _(b):
        INN[...] = nt(DO[rows(b)], wout[...])
        COL[...] = jnp.zeros(COL.shape, f32)

        @pl.loop(0, n // RT)
        def _(i):
            r = pl.ds(pl.multiple_of(i * RT, RT), RT)
            o = pl.ds(pl.multiple_of(b * n + i * RT, RT), RT)
            lane = lax.broadcasted_iota(jnp.int32, (RT, 128), 1)
            col = jnp.zeros((RT, 128), f32)
            for e in range(experts):
                v = INN[r, e * U : (e + 1) * U]
                a = ACT[o, e * U : (e + 1) * U].astype(f32)
                col = jnp.where(lane == e, jnp.sum(a * v, axis=-1, keepdims=True), col)
                DIN[o, e * U : (e + 1) * U] = (DG[o, e * U : (e + 1) * U] * v).astype(bf16)
            COL[r] = col

        DW[b] = COL[...].T[0:8]
        PO[rows(b)] = nn(ACT[rows(b)], wout[...]).astype(bf16)
        PH[rows(b)] = nt(DIN[rows(b)], win[...]).astype(bf16)

    Ds = D // g.S
    for e in range(experts):
        v = tn(H[...], DIN[:, e * U : (e + 1) * U])
        for s in range(g.S):
            j = lax.rem(s - w.s + g.S, g.S)
            for u in range(Ds // g.CR):
                lo = s * Ds + u * g.CR
                GI[(j * experts + e) * (Ds // g.CR) + u] = v[lo : lo + g.CR]


def scatter_group(w, sends, PB, bufs, sems, n, n0):
    g = w.g
    RC, RXA, RSA, RSB, RXB = bufs
    cs, xas, sas, sbs, xbs = sems
    n1 = n - n0

    def blk(js, jx, jc, lo=0, size=n):
        return pl.ds(pl.multiple_of(w.block(js, jx, jc) * n + lo, 16), size)

    order = [(js, jx) for js in reversed(range(g.S)) for jx in reversed(range(g.X))]
    if g.C > 1:
        for js, jx in order:
            q = w.sj(js) * g.X + w.xj(jx)
            sends.go(PB.at[blk(js, jx, 1)], RC.at[q], cs.at[q], w.dev(jc=1))
        for js, jx in order:
            q = w.sj(js) * g.X + w.xj(jx)
            arrived(RC.at[q], cs.at[q])
            r = blk(js, jx, 0)
            PB[r] = (PB[r].astype(f32) + RC[q].astype(f32)).astype(bf16)
            if jx:
                d = RXA.at[jx - 1, w.sj(js)]
                sends.go(PB.at[blk(js, jx, 0, 0, n0)], d, xas.at[jx - 1, w.sj(js)], w.dev(jx=jx))
            if js:
                d = RSB.at[js - 1, w.xj(jx)]
                sends.go(PB.at[blk(js, jx, 0, n0, n1)], d, sbs.at[js - 1, w.xj(jx)], w.dev(js=js))
    else:
        for js, jx in order:
            if jx:
                d = RXA.at[jx - 1, w.sj(js)]
                sends.go(PB.at[blk(js, jx, 0, 0, n0)], d, xas.at[jx - 1, w.sj(js)], w.dev(jx=jx))
            if js:
                d = RSB.at[js - 1, w.xj(jx)]
                sends.go(PB.at[blk(js, jx, 0, n0, n1)], d, sbs.at[js - 1, w.xj(jx)], w.dev(js=js))
    for js in reversed(range(g.S)):
        r = blk(js, 0, 0, 0, n0)
        v = PB[r].astype(f32)
        for jx in range(1, g.X):
            arrived(RXA.at[jx - 1, w.sj(js)], xas.at[jx - 1, w.sj(js)])
            v = v + RXA[jx - 1, w.sj(js)].astype(f32)
        if js:
            PB[r] = v.astype(bf16)
            sends.go(PB.at[r], RSA.at[js - 1], sas.at[js - 1], w.dev(js=js))
        else:
            top = v
    for jx in reversed(range(g.X)):
        r = blk(0, jx, 0, n0, n1)
        v = PB[r].astype(f32)
        for js in range(1, g.S):
            arrived(RSB.at[js - 1, w.xj(jx)], sbs.at[js - 1, w.xj(jx)])
            v = v + RSB[js - 1, w.xj(jx)].astype(f32)
        if jx:
            PB[r] = v.astype(bf16)
            sends.go(PB.at[r], RXB.at[jx - 1], xbs.at[jx - 1], w.dev(jx=jx))
        else:
            low = v
    for js in range(1, g.S):
        arrived(RSA.at[js - 1], sas.at[js - 1])
        top = top + RSA[js - 1].astype(f32)
    for jx in range(1, g.X):
        arrived(RXB.at[jx - 1], xbs.at[jx - 1])
        low = low + RXB[jx - 1].astype(f32)
    return top, low


def scatter_scratch(g, n, n0, width):
    n1 = n - n0
    sm1, xm1 = max(1, g.S - 1), max(1, g.X - 1)
    dma = pltpu.SemaphoreType.DMA
    return (
        [
            pltpu.VMEM((g.S * g.X, n, width), bf16),
            pltpu.VMEM((xm1, g.S, n0, width), bf16),
            pltpu.VMEM((sm1, n0, width), bf16),
            pltpu.VMEM((sm1, g.X, n1, width), bf16),
            pltpu.VMEM((xm1, n1, width), bf16),
        ],
        [dma((g.S * g.X,)), dma((xm1, g.S)), dma((sm1,)), dma((sm1, g.X)), dma((xm1,))],
    )


def attention_back(proj, probs, dattn, dproj, g):
    D = dattn.shape[1]
    low = lax.broadcasted_iota(jnp.int32, (1, 128), 1) < HEAD_DIM
    zero = jnp.zeros((), bf16)
    scale = HEAD_DIM**-0.5
    for p in range(D // 128):
        q2 = proj[0 : g.TP, p * 128 : (p + 1) * 128] * jnp.asarray(scale, bf16)
        k2 = proj[:, D + p * 128 : D + (p + 1) * 128]
        v2 = proj[:, 2 * D + p * 128 : 2 * D + (p + 1) * 128]
        d2 = dattn[:, p * 128 : (p + 1) * 128]
        dq = dk = dv = None
        for i in range(2):
            mine = low if i == 0 else jnp.logical_not(low)
            pr = probs[2 * p + i]
            da = jnp.where(mine, d2, zero)
            dp = nt(da, v2)
            ds = (pr * (dp - jnp.sum(dp * pr, axis=-1, keepdims=True))).astype(bf16)
            a = nn(ds, jnp.where(mine, k2, zero))
            b = tn(ds, jnp.where(mine, q2, zero))
            c = tn(pr.astype(bf16), da)
            dq, dk, dv = (a, b, c) if i == 0 else (dq + a, dk + b, dv + c)
        dproj[:, p * 128 : (p + 1) * 128] = (dq * scale).astype(bf16)
        dproj[:, D + p * 128 : D + (p + 1) * 128] = dk[0 : g.TP].astype(bf16)
        dproj[:, 2 * D + p * 128 : 2 * D + (p + 1) * 128] = dv[0 : g.TP].astype(bf16)


class Chain:
    def __init__(self, w, n, own, bufs, sems):
        self.w, self.n, self.own = w, n, own
        self.RU, self.RD, self.SU, self.SD, self.tot = bufs
        self.ru, self.rd, self.su, self.sd = sems
        g = w.g
        self.up, self.down = w.red, g.L - 1 - w.red
        self.most = jnp.maximum(self.up, self.down)

    def _copy(self, k, upward):
        w, g = self.w, self.w.g
        src, dst, ss, rs, d = (self.SU, self.RU, self.su, self.ru, g.T) if upward else (self.SD, self.RD, self.sd, self.rd, -g.T)
        return pltpu.make_async_remote_copy(
            src_ref=src.at[k], dst_ref=dst.at[k], send_sem=ss.at[k], recv_sem=rs.at[k],
            device_id=(w.rep + d, w.s), device_id_type=MESH,
        )

    def step(self, i, lag):
        for upward in (True, False):
            behind, ahead = (self.up, self.down) if upward else (self.down, self.up)
            R, sem, S = (self.RU, self.ru, self.SU) if upward else (self.RD, self.rd, self.SD)
            k = i - lag * behind
            ok = (k >= 0) & (k < self.n)

            @pl.when(ok & (behind > 0))
            def _():
                arrived(R.at[k], sem.at[k])

            @pl.when(ok & (behind > 0) & (ahead > 0))
            def _():
                S[k] = (self.own(k) + R[k].astype(f32)).astype(bf16)

            @pl.when(ok & (behind == 0) & (ahead > 0))
            def _():
                S[k] = self.own(k).astype(bf16)

            @pl.when(ok & (ahead > 0))
            def _():
                self._copy(k, upward).start()

    def total(self, k, store):
        self.tot[...] = self.own(k)

        @pl.when(self.up > 0)
        def _():
            self.tot[...] += self.RU[k].astype(f32)

        @pl.when(self.down > 0)
        def _():
            self.tot[...] += self.RD[k].astype(f32)

        store(self.tot[...].astype(bf16))

    def finish(self):
        @pl.loop(0, self.n)
        def _(k):
            @pl.when(self.down > 0)
            def _():
                self._copy(k, True).wait_send()

            @pl.when(self.up > 0)
            def _():
                self._copy(k, False).wait_send()


def back(g, experts, ins, outs, scr):
    w = Where(g)
    (PO, PH, DW, GO, GI, mixed, proj, attn, probs, tok, cot, WM, smallf, wqkv, wattn) = ins
    out, gtok, gqkv, gattn, gsmall, gin_h, gout_h = outs
    (PHs, POs, DWr, dattn, dproj, M, dmix, FM, FO, FI, chain_b, mchain_b, rs_h, rs_o, rs_m, stage, ssem, wsem, fsem, lsem, chain_s, mchain_s, ph_s, po_s, m_s) = scr
    D = tok.shape[2]
    n = g.TP
    n0 = n // 32 * 16
    Ds = D // g.S
    U = g.U
    CR = g.CR
    L = g.L
    greet(w, True)
    sends = Sends(ssem)
    for js in range(g.S):
        for jx in range(g.X):
            for jc in range(g.C):
                if js or jx or jc:
                    sends.go(DW.at[w.block(js, jx, jc)], DWr.at[w.tp], wsem.at[w.tp], w.dev(js, jx, jc))
    cp1 = pltpu.make_async_copy(PH, PHs, lsem.at[0])
    cp1.start()
    cp2 = pltpu.make_async_copy(PO, POs, lsem.at[1])
    cp2.start()
    cp1.wait()
    dh_top, dh_low = scatter_group(w, sends, PHs, rs_h, ph_s, n, n0)
    dh2 = jnp.concatenate([dh_top, dh_low], axis=0)
    gdg = DW[w.tp]
    for js in range(g.S):
        for jx in range(g.X):
            for jc in range(g.C):
                if js or jx or jc:
                    b = w.block(js, jx, jc)
                    arrived(DWr.at[b], wsem.at[b])
                    gdg = gdg + DWr[b]
    small = smallf[...]
    small_rows = rows_of_small(small)
    gain_one = small_rows[experts : experts + 1]
    gain_two = small_rows[experts + 1 : experts + 2]
    dlt = gdg - WM[w.tp] * jnp.sum(gdg, axis=0, keepdims=True)
    dl = turned(dlt)[0:n]
    da, db, dc = split3(dl)
    dh2 = dh2 + nt(da, small) + nt(db, small) + nt(dc, small)
    h2, xhat2, r2 = layer_norm(mixed[...], gain_two)
    ha, hb, _ = split3(h2)
    ggate = tn(ha, da) + tn(hb, da) + tn(ha, db)
    gtwo = jnp.sum(dh2 * xhat2, axis=0, keepdims=True)
    dmixed = padded(cot, n) + norm_back(dh2, xhat2, r2, gain_two)
    dmix[...] = dmixed
    dlow = dmixed.astype(bf16)
    dattn[...] = nt(dlow, wattn[...]).astype(bf16)
    M[:, 3 * D : 4 * D] = tn(attn[...], dlow).astype(bf16)
    attention_back(proj, probs, dattn, dproj, g)
    h1, xhat1, r1 = layer_norm(padded(tok, n), gain_one)
    h1b = h1.astype(bf16)
    for k in range(3):
        M[:, k * D : (k + 1) * D] = tn(h1b, dproj[:, k * D : (k + 1) * D]).astype(bf16)
    dh1 = nt(dproj[...], wqkv[...])
    gone = jnp.sum(dh1 * xhat1, axis=0, keepdims=True)
    gtok[0] = (dmix[...] + norm_back(dh1, xhat1, r1, gain_one))[0 : g.seq].astype(bf16)
    rows8 = jnp.concatenate([jnp.zeros((experts, D), f32), gone, gtwo, jnp.zeros((126 - experts, D), f32)], axis=0)
    M[:, 4 * D :] = (ggate + rows8.T).astype(bf16)
    cp2.wait()
    o_top, o_low = scatter_group(w, sends, POs, rs_o, po_s, n, n0)
    out[0] = (mixed[...] + jnp.concatenate([o_top, o_low], axis=0))[0 : g.seq].astype(bf16)
    nm = D // GROUP
    m_top, m_low = scatter_group(w, sends, M, rs_m, m_s, nm, nm // 2)
    mown = mchain_b[5]
    q = nm // 4
    mown[0] = m_top[0:q]
    mown[1] = m_top[q:]
    mown[2] = m_low[0:q]
    mown[3] = m_low[q:]

    NO = GO.shape[0]
    NI = GI.shape[0]
    per_j = NI // g.S
    cu, cc = U // CR, D // 256
    ci = Ds // CR

    def own(k):
        return G_all[k]

    G_all = chain_b[5]
    cpo = pltpu.make_async_copy(GO, G_all.at[pl.ds(0, NO)], lsem.at[2])
    cpi = pltpu.make_async_copy(GI, G_all.at[pl.ds(NO, NI)], lsem.at[3])
    cpo.start()
    cpi.start()
    cpo.wait()
    cpi.wait()
    ch = Chain(w, NO + NI, own, chain_b[:5], chain_s)
    lag = 2

    def out_view(k, t):
        e, r = k // (cu * cc), lax.rem(k, cu * cc)
        return FO.at[
            e,
            pl.ds(pl.multiple_of(t * U + (r // cc) * CR, 16), CR),
            pl.ds(pl.multiple_of(lax.rem(r, cc) * 256, 256), 256),
        ]

    def in_view(k, tp):
        e, u = k // ci, lax.rem(k, ci)
        return FI.at[e, pl.ds(pl.multiple_of(u * CR, 16), CR), pl.ds(pl.multiple_of(tp * U, 128), U)]

    def put(view, sem_at, jx, jc):
        cp = pltpu.make_async_remote_copy(
            src_ref=view, dst_ref=view, send_sem=fsem.at[2, 0, 0], recv_sem=sem_at, device_id=w.dev(0, jx, jc), device_id_type=MESH
        )
        cp.start()
        cp.wait_send()

    def spread(view, sem_at):
        for jx in range(1, g.X):
            put(view, sem_at, jx, 0)
        for jc in range(1, g.C):
            put(view, sem_at, 0, jc)

    def relay(view, sem_at):
        arrived(view, sem_at)
        for jc in range(1, g.C):
            put(view, sem_at, 0, jc)

    steps = NO + NI + lag * (L - 1)

    @pl.loop(0, steps)
    def _(i):
        ch.step(i, lag)
        k = i - lag * ch.most

        @pl.when((k >= 0) & (k < NO))
        def _():
            view = out_view(k, w.t)

            def store(v):
                view[...] = v

            ch.total(k, store)
            spread(view, fsem.at[0, w.tp, k])

        @pl.when((k >= NO) & (k < NO + NI))
        def _():
            j = (k - NO) // per_j
            kk = lax.rem(k - NO, per_j)
            view = in_view(kk, w.tp)
            SI = stage

            def store(v):
                SI[lax.rem(k, 2)] = v

            ch.total(k, store)
            src = SI.at[lax.rem(k, 2)]

            @pl.when(j == 0)
            def _():
                view[...] = src[...]
                spread(view, fsem.at[1, w.tp, kk])

            @pl.when(j > 0)
            def _():
                cp = pltpu.make_async_remote_copy(
                    src_ref=src, dst_ref=view, send_sem=fsem.at[2, 0, 0], recv_sem=fsem.at[1, w.tp, kk],
                    device_id=(w.rep, lax.rem(w.s + j, g.S)), device_id_type=MESH,
                )
                cp.start()
                cp.wait_send()

    for j in range(1, g.S):
        b = w.block(j, 0, 0)

        @pl.loop(0, per_j)
        def _(k):
            view = in_view(k, b)
            arrived(view, fsem.at[1, b, k])
            spread(view, fsem.at[1, b, k])

    for jx in range(1, g.X):
        b = w.block(0, jx, 0)
        t = w.xj(jx) * g.C + w.c

        @pl.loop(0, NO)
        def _(k):
            relay(out_view(k, t), fsem.at[0, b, k])

        for j in range(g.S):
            b = w.block(j, jx, 0)

            @pl.loop(0, per_j)
            def _(k):
                relay(in_view(k, b), fsem.at[1, b, k])

    for jc in range(1, g.C):
        for jx in range(g.X):
            t = w.xj(jx) * g.C + w.cj(jc)
            b = w.block(0, jx, jc)

            @pl.loop(0, NO)
            def _(k):
                arrived(out_view(k, t), fsem.at[0, b, k])

            for j in range(g.S):
                b = w.block(j, jx, jc)

                @pl.loop(0, per_j)
                def _(k):
                    arrived(in_view(k, b), fsem.at[1, b, k])

    mch = Chain(w, 4, lambda k: mown[k], mchain_b[:5], mchain_s)

    def m_view(t, k):
        return FM.at[pl.ds(pl.multiple_of(t * nm + k * q, 16), q)]

    @pl.loop(0, 4 + L - 1)
    def _(i):
        mch.step(i, 1)
        k = i - mch.most

        @pl.when((k >= 0) & (k < 4))
        def _():
            view = m_view(w.t, k)

            def store(v):
                view[...] = v

            mch.total(k, store)
            spread(view, fsem.at[3, w.t, k])

    for jx in range(1, g.X):
        t = w.xj(jx) * g.C + w.c

        @pl.loop(0, 4)
        def _(k):
            relay(m_view(t, k), fsem.at[3, t, k])

    for jc in range(1, g.C):
        for jx in range(g.X):
            t = w.xj(jx) * g.C + w.cj(jc)

            @pl.loop(0, 4)
            def _(k):
                arrived(m_view(t, k), fsem.at[3, t, k])

    gqkv[...] = FM[:, 0 : 3 * D].astype(f32)
    gattn[...] = FM[:, 3 * D : 4 * D].astype(f32)
    gsmall[...] = FM[:, 4 * D :].astype(f32)
    for e in range(experts):
        gout_h[e] = FO[e].astype(f32)
        gin_h[e] = FI[e].astype(f32)
    ch.finish()
    mch.finish()
    sends.finish()


def on_device(mesh, tokens, norm_one, w_qkv, w_attn, norm_two, w_gate, w_expin, w_expout, routes, cotangent):
    g = geometry(mesh, tokens.shape, w_expout.shape[1] * mesh.shape["shard"])
    experts = w_expin.shape[0]
    D = tokens.shape[2]
    Ds = D // g.S
    U = g.U
    n = g.TP
    N = GROUP * n
    EU = experts * U
    dma = pltpu.SemaphoreType.DMA
    vm = pl.BlockSpec(memory_space=pltpu.VMEM)
    hb = pl.BlockSpec(memory_space=pl.ANY)
    sds = jax.ShapeDtypeStruct
    small = jnp.concatenate(
        [w_gate, norm_one[:, None], norm_two[:, None], jnp.zeros((Ds, 126 - experts), bf16)], axis=1
    )
    front_out = [
        sds((N, D), bf16), sds((N, D), bf16), sds((GROUP, 8, g.TK), f32), sds((D, EU), bf16), sds((D, 3 * D), bf16),
        sds((D, D), bf16), sds((D, 128), bf16), sds((g.TK, 3 * D), bf16), sds((n, D), bf16),
        sds((HEADS, n, g.TK), f32), sds((n, D), f32),
    ]

    def body1(*refs):
        front(g, experts, refs[:7], refs[7:18], refs[18:])

    H, DO, WM, win, wqkv, wattn, smallf, proj, attn, probs, mixed = pl.pallas_call(
        body1,
        name="front",
        out_shape=front_out,
        in_specs=[vm, vm, vm, vm, hb, hb, hb],
        out_specs=[vm] * len(front_out),
        scratch_shapes=[dma((96,)), dma((3, g.S, g.C)), dma((GROUP, 2)), dma((GROUP, 2)), dma((GROUP,)), dma((8 + g.S * experts,))],
        compiler_params=pltpu.CompilerParams(collective_id=0, has_side_effects=True, vmem_limit_bytes=VMEM_BYTES),
    )(tokens, cotangent, routes, small, w_qkv, w_attn, w_expin)

    NO = experts * (U // g.CR) * (D // 256)
    NI = g.S * experts * (Ds // g.CR)
    mid_out = [sds((N, D), bf16), sds((N, D), bf16), sds((GROUP, 8, g.TK), f32), sds((NO, g.CR, 256), f32), sds((NI, g.CR, U), f32)]

    def body2(*refs):
        middle(g, experts, refs[:5], refs[5:10], refs[10:])

    PO, PH, DW, GO, GI = pl.pallas_call(
        body2,
        name="middle",
        out_shape=mid_out,
        in_specs=[vm, vm, vm, vm, hb],
        out_specs=[vm] * len(mid_out),
        scratch_shapes=[
            pltpu.VMEM((EU, D), bf16), pltpu.VMEM((n, EU), f32), pltpu.VMEM((N, EU), bf16), pltpu.VMEM((N, EU), f32),
            pltpu.VMEM((N, EU), bf16), pltpu.VMEM((g.TK, 128), f32), dma((experts,)),
        ],
        compiler_params=pltpu.CompilerParams(vmem_limit_bytes=VMEM_BYTES),
    )(H, DO, WM, win, w_expout)

    nm = D // GROUP
    MW = 4 * D + 128
    rs_h, ph_s = scatter_scratch(g, n, n // 32 * 16, D)
    rs_o, po_s = scatter_scratch(g, n, n // 32 * 16, D)
    rs_m, m_s = scatter_scratch(g, nm, nm // 2, MW)
    NC = NO + NI
    chain_b = [pltpu.VMEM((NC, g.CR, 256), bf16)] * 4 + [pltpu.VMEM((g.CR, 256), f32), pltpu.VMEM((NC, g.CR, 256), f32)]
    mchain_b = [pltpu.VMEM((4, nm // 4, MW), bf16)] * 4 + [pltpu.VMEM((nm // 4, MW), f32), pltpu.VMEM((4, nm // 4, MW), f32)]
    flat = [
        pltpu.VMEM((N, D), bf16), pltpu.VMEM((N, D), bf16), pltpu.VMEM((GROUP, 8, g.TK), f32), pltpu.VMEM((n, D), bf16),
        pltpu.VMEM((n, 3 * D), bf16), pltpu.VMEM((D, MW), bf16), pltpu.VMEM((n, D), f32), pltpu.VMEM((Ds, MW), bf16),
        pltpu.VMEM((experts, U * g.T, D), bf16), pltpu.VMEM((experts, Ds, U * GROUP), bf16),
        chain_b, mchain_b, rs_h, rs_o, rs_m,
        pltpu.VMEM((2, g.CR, 256), bf16), dma((96,)), dma((GROUP,)), dma((4, GROUP, max(NO, NI))), dma((4,)),
        [dma((NC,))] * 4, [dma((4,))] * 4, ph_s, po_s, m_s,
    ]
    leaves, tree = jax.tree.flatten(flat, is_leaf=lambda v: not isinstance(v, list))
    back_out = [
        sds(tokens.shape, bf16), sds(tokens.shape, bf16), sds((Ds, 3 * D), f32), sds((Ds, D), f32), sds((Ds, 128), f32),
        sds(w_expin.shape, f32), sds(w_expout.shape, f32),
    ]

    def body3(*refs):
        back(g, experts, refs[:15], refs[15:22], jax.tree.unflatten(tree, refs[22:]))

    out, gtok, gqkv, gattn, gsmall, gin, gout = pl.pallas_call(
        body3,
        name="back",
        out_shape=back_out,
        in_specs=[hb, hb, vm, hb, hb] + [vm] * 10,
        out_specs=[vm] * 5 + [vm, vm],
        scratch_shapes=leaves,
        compiler_params=pltpu.CompilerParams(collective_id=1, has_side_effects=True, vmem_limit_bytes=VMEM_BYTES),
    )(PO, PH, DW, GO, GI, mixed, proj, attn, probs, tokens, cotangent, WM, smallf, wqkv, wattn)
    return (
        out, gtok, gsmall[:, experts], gqkv, gattn, gsmall[:, experts + 1], gsmall[:, :experts], gin, gout,
    )


def solution(mesh):
    placed = (
        P(("rep", "shard"), None, None), P("shard"), P("shard", None), P("shard", None), P("shard"), P("shard", None),
        P(None, "shard", None), P(None, "shard", None), P(("rep", "shard"), None, None), P(("rep", "shard"), None, None),
    )
    return jax.shard_map(
        partial(on_device, mesh),
        mesh=mesh,
        in_specs=placed,
        out_specs=(
            P(("rep", "shard"), None, None), P(("rep", "shard"), None, None), P("shard"), P("shard", None),
            P("shard", None), P("shard"), P("shard", None), P(None, "shard", None), P(None, "shard", None),
        ),
        check_vma=False,
    )
```

time: 765 us -> 373 us (0.49)
  waiting for transfers between devices: 576 us -> 0 us
  Pallas kernels: 0 us -> 345 us
  matrix products: 74.1 us -> 0 us
  blocking collectives: 67.2 us -> 0 us
  other arithmetic: 18.4 us -> 0.74 us
  between operations: 14.8 us -> 0.7 us
  local copies, waits for them, and re-layouts: 13.1 us -> 25.8 us
    pallas_call x0 -> x3, Pallas kernels: none -> 345 us  [the longest x1 246 us: on_device(): pl.pallas_call(body3, name='back', out_shape=back_out, in_specs=[hb, hb,...]
    reduce_scatter x4 -> x0, waiting for transfers between devices: 224 us -> none  [the longest x1 102 us: on_device(): lax.psum_scatter(grad_expout.astype(jnp.bfloat16), 'shard', scatter_dimen...]
    all_gather x3 -> x0, waiting for transfers between devices: 193 us -> none  [the longest x1 99.3 us: on_device(): lax.all_gather(w_expin, 'shard', axis=1, tiled=True)]
    psum x1 -> x0, waiting for transfers between devices: 153 us -> none  [on_device(): lax.psum(owned[5].astype(jnp.bfloat16), 'rep').astype(jnp.float32)]
    dot_general x21 -> x0, matrix products: 74.1 us -> none  [the longest x1 18.8 us: forward(): jnp.einsum('td,edf->etf', hidden_two_low, w_expin, preferred_element_type...]
    psum x1 -> x0, blocking collectives: 34.5 us -> none  [on_device(): lax.psum(owned[0].astype(jnp.bfloat16), 'rep').astype(jnp.float32)]
    all_gather x4 -> x0, blocking collectives: 27.8 us -> none  [the longest x1 14 us: on_device(): lax.all_gather(w_attn, 'shard', axis=0, tiled=True)]
    convert_element_type x12 -> x0, other arithmetic: 16.5 us -> none  [the longest x1 6.77 us: on_device(): lax.psum(owned[6].astype(jnp.bfloat16), 'rep').astype(jnp.float32)]
  transfers between devices with their start and end apart: 9 -> 0, of which waited for: 8 -> 0; matrix products, arithmetic and copies ran while one was open for 7% -> 0% of each run, Pallas kernels for 0% -> 0%
where the time goes in v1:
time: 373 us; the launch traced here: 372 us
  Pallas kernels  345 us (92%)
  local copies, waits for them, and re-layouts  25.8 us (7%)
    pallas_call x1, Pallas kernels, on_device(): pl.pallas_call(body3, name='back', out_shape=back_out, in_specs=[hb, hb,...  246 us
    pallas_call x1, Pallas kernels, on_device(): pl.pallas_call(body1, name='front', out_shape=front_out, in_specs=[vm, vm...  61 us
    pallas_call x1, Pallas kernels, on_device(): pl.pallas_call(body2, name='middle', out_shape=mid_out, in_specs=[vm, vm,...  37.7 us
    unnamed x15, local copies, waits for them, and re-layouts  22.5 us

profile of v1, /device:TPU:0, one launch (start us, length us, event | category | flops | bytes accessed | tf_op | source)
XLA Modules:
  0.0 372.4 jit_solution(13628155284319570091)
XLA Ops:
  0.7 0.1 pad.3.clone
  0.7 0.7 broadcast_in_dim.12
  1.5 0.8 broadcast_in_dim.13
  2.2 0.8 copy.22
  3.1 0.7 maximum_maximum_fusion.refs_3_
  3.8 1.4 copy.25.refs_2_
  5.3 61.0 %front.1 = (bf16[1664,512]{1,0:T(8,128)(2,1)}, bf16[1664,512]{1,0:T(8,128)(2,1)}, f32[8,8,256]{2,1,0:T(8,128)}, bf16[512,1024]{1,0:T(8,128)(2,1)}, bf16[512,1536...) custom-call(bf16[1,197,512]{2,1,0:T(8,128)(2,1)} %refs_9_.1, ...), custom_call_target="tpu_custom_call" | custom-call | tf_op jit(solution)/shard_map/front/pallas_call | solution.py:914
  66.3 37.7 %middle.1 = (bf16[1664,512]{1,0:T(8,128)(2,1)}, bf16[1664,512]{1,0:T(8,128)(2,1)}, f32[8,8,256]{2,1,0:T(8,128)}, f32[16,128,256]{2,1,0:T(8,128)}, f32[16,128,256]{2,1,0:T(8,128)}) custom-call(bf16[1664,512]{1,0:T(8,128)(2,1)} %get-tuple-element.32.refs_0_, bf16[1664,512]{1,0:T(8,128)(2,1)} %get-tuple-element.33.refs_1_, ...), custom_call_target="tpu_custom_call" | custom-call | tf_op jit(solution)/shard_map/middle/pallas_call | solution.py:931
  104.0 246.4 %back.1 = (bf16[1,197,512]{2,1,0:T(8,128)(2,1)}, bf16[1,197,512]{2,1,0:T(8,128)(2,1)}, f32[256,1536]{1,0:T(8,128)}, f32[256,512]{1,0:T(8,128)}, f32[256,128]{1,0...) custom-call(bf16[1664,512]{1,0:T(8,128)(2,1)} %get-tuple-element.36.refs_0_, ...), custom_call_target="tpu_custom_call" | custom-call | tf_op jit(solution)/shard_map/back/pallas_call | solution.py:969
  350.4 1.8 slice_reduce_fusion
  352.2 0.0 copy-start
  352.2 1.6 copy.26
  353.9 1.6 copy.33
  355.5 1.6 copy.34
  357.1 2.7 copy.35
  359.8 0.0 copy-done
  359.8 0.0 slice-start
  359.8 0.8 copy.36
  360.6 0.0 slice-start.1
  360.6 8.5 %copy.37 = f32[4,256,2048]{2,1,0:T(8,128)} copy(f32[4,256,2048]{2,1,0:T(8,128)} %get-tuple-element.91) | data formatting | bytes 16777216
  369.0 0.0 slice-done
  369.0 0.0 slice-done.1
  369.0 3.4 copy.38
  (2 shorter events, 0.0 us)
Async XLA Ops:
  352.2 7.5 %copy-start = (f32[256,512]{1,0:T(8,128)S(1)}, f32[256,512]{1,0:T(8,128)}, u32[]{:S(2)}) copy-start(f32[256,512]{1,0:T(8,128)} %get-tuple-element.88) | copy-start | bytes 1572868
  359.8 9.3 %slice-start = ((s8[8388608]{0:T(1024)(128)(4,1)}), s8[4194304]{0:T(1024)(128)(4,1)S(1)}, s32[]{:S(2)}) async-start(s8[8388608]{0:T(1024)(128)(4,1)} %bitcast.1), calls=%async_computation | async-start | bytes 8388608
  360.6 8.5 %slice-start.1 = ((s8[8388608]{0:T(1024)(128)(4,1)}), s8[4194304]{0:T(1024)(128)(4,1)S(1)}, s32[]{:S(2)}) async-start(s8[8388608]{0:T(1024)(128)(4,1)} %bitcast.1), calls=%async_computation.1 | async-start | bytes 8388608
